TPU v7x, 32 devices: a whole 2x2x4 slice. The times are simulated.
32 devices in a mesh: stn: 16 (over z, y, core), pol: 2 (over x).
Axes of the slice: x: 2, y: 2, z: 4, core: 2. Of those that a mesh axis runs over, the one named last changes fastest.
Arguments:
- voltages: bfloat16 [64, 2, 2, 132992], P('stn', 'pol'), may hold values from -6 to 6, as said below
- delay_table: int32 [64], P('stn'), may hold values from 0 to 128
- channel_map: int32 [256], replicated, may hold values from 0 to 255, each once
- row_assign: int32 [32], replicated, may hold values from 0 to 31, each once
Outputs:
- bandpass: float32 [256, 128], P(('stn', 'pol'))
- lags: bfloat16 [32, 2, 256, 4, 128], P(('stn', 'pol'))
- delays: float32 [32, 4, 128], P(('stn', 'pol'))
Inputs may be any that keep to these rules, and one draw needn't show every extreme that they name: `voltages`: A station's two polarizations and its real and imaginary parts are noisy copies of common signals with station-dependent time shifts. `channel_map`: each channel appears in exactly one slot. `row_assign`: each row block appears in exactly one slot.
All inputs are finite; a program needn't handle non-finite values.
Results may differ from a plain program's by a relative error of at most 0.0059.
Values may be sent and summed in bfloat16 or wider, within the bound.
A program may use at most 128 MiB of HBM per device.

v0:
```python
import math
import jax
import jax.numpy as jnp
from jax import lax
from jax.sharding import PartitionSpec as P

CHANNELS = 256
TAPS = 8
SPECTRA = 512


def prototype():
    tap_total = TAPS * CHANNELS
    sample_index = jnp.arange(tap_total, dtype=jnp.float32)
    taper_values = 0.5 - 0.5 * jnp.cos(2.0 * math.pi * (sample_index + 0.5) / tap_total)
    offset = (sample_index - (tap_total - 1) / 2.0) / CHANNELS
    values = jnp.sin(math.pi * offset) / (math.pi * offset) * taper_values
    values = values * jnp.sqrt(CHANNELS / jnp.sum(values * values))
    return values.reshape(TAPS, CHANNELS)


def phase_parts(channels):
    cell_index = jnp.arange(CHANNELS, dtype=jnp.int32)
    phase_turns = channels[:, None] * cell_index[None, :] % CHANNELS
    phase_angle = phase_turns.astype(jnp.float32) * (2.0 * math.pi / CHANNELS)
    scale_factor = 1.0 / math.sqrt(CHANNELS)
    return (jnp.cos(phase_angle) * scale_factor, jnp.sin(phase_angle) * scale_factor)


def channel_table(channels):
    cosine, sine_part = phase_parts(channels)
    forward = jnp.stack([jnp.stack([cosine, sine_part], 1), jnp.stack([-sine_part, cosine], 1)], 0)
    return forward.astype(jnp.bfloat16)


def lag_table(channels):
    cosine, sine_part = phase_parts(channels)
    cosine = cosine.T
    sine_part = sine_part.T
    backward = jnp.stack([jnp.stack([cosine, -sine_part], 2), jnp.stack([sine_part, cosine], 2)], 0)
    return backward.astype(jnp.bfloat16)


def filter_bank(segment, window):
    framed = segment.reshape(segment.shape[:-1] + (SPECTRA + TAPS - 1, CHANNELS))
    total = jnp.zeros(segment.shape[:-1] + (SPECTRA, CHANNELS), jnp.float32)
    for tap_index in range(TAPS):
        total = (
            total
            + framed[..., tap_index : tap_index + SPECTRA, :].astype(jnp.float32)
            * window[tap_index]
        )
    return total.astype(jnp.bfloat16)


def per_device(voltages, delay_table, channel_map, row_assign):
    stn_count = lax.axis_size("stn")
    pol_count = lax.axis_size("pol")
    owner_count = stn_count * pol_count
    local_channels = CHANNELS // owner_count
    span = (SPECTRA + TAPS - 1) * CHANNELS
    window = prototype()
    position = jnp.arange(CHANNELS, dtype=jnp.int32)
    forward = channel_table(jnp.take(channel_map, position))

    def cut_segment(station_volts, start_sample):
        return lax.dynamic_slice_in_dim(station_volts, start_sample, span, 2)

    segment = jax.vmap(cut_segment)(voltages, delay_table)
    filtered = filter_bank(segment, window)
    spectra = jnp.einsum(
        "qkpc,tapsc->taqks", forward, filtered, preferred_element_type=jnp.float32
    ).astype(jnp.bfloat16)
    turned = lax.all_to_all(
        lax.all_to_all(spectra, "stn", split_axis=3, concat_axis=0, tiled=True),
        "pol",
        split_axis=3,
        concat_axis=1,
        tiled=True,
    )
    input_count = 2 * turned.shape[0]

    def correlate(channel_slot):
        channel_block = lax.dynamic_index_in_dim(turned, channel_slot, 3, keepdims=False)
        real_part = channel_block[:, :, 0].reshape(input_count, SPECTRA)
        imag_part = channel_block[:, :, 1].reshape(input_count, SPECTRA)
        stacked = jnp.concatenate([real_part, imag_part], 1)
        rotated = jnp.concatenate([-imag_part, real_part], 1)
        partner = jnp.concatenate([stacked, rotated], 0)
        product = (
            lax.dot_general(
                stacked, partner, (((1,), (1,)), ((), ())), preferred_element_type=jnp.float32
            )
            / SPECTRA
        )
        vis_real = product[:, :input_count]
        vis_imag = product[:, input_count:]
        return (jnp.stack([vis_real, vis_imag]).astype(jnp.bfloat16), jnp.diagonal(vis_real))

    visibility, bandpass = lax.map(correlate, jnp.arange(local_channels, dtype=jnp.int32))
    row_block = input_count // owner_count
    blocked = visibility.reshape(local_channels, 2, owner_count, row_block, input_count)
    block_index = jnp.arange(owner_count, dtype=jnp.int32)
    arranged = jnp.take(blocked, jnp.take(row_assign, block_index), axis=2)
    arranged = arranged.reshape(1, 1, local_channels, 2, input_count, input_count)
    regrouped = lax.all_to_all(
        lax.all_to_all(arranged, "stn", split_axis=4, concat_axis=0, tiled=True),
        "pol",
        split_axis=4,
        concat_axis=1,
        tiled=True,
    )
    gathered = regrouped.reshape(CHANNELS, 2, row_block * input_count)
    backward = lag_table(channel_map)
    lag = jnp.einsum("qlkp,kpm->qlm", backward, gathered, preferred_element_type=jnp.float32)
    power = lag[0] * lag[0] + lag[1] * lag[1]
    lag_position = jnp.where(position < CHANNELS // 2, position, position - CHANNELS).astype(
        jnp.float32
    ) / (CHANNELS // 2)
    delay = jnp.sum(power * lag_position[:, None], 0) / (jnp.sum(power, 0) + 1e-06)
    lags = lag.astype(jnp.bfloat16).reshape(1, 2, CHANNELS, row_block, input_count)
    delays = delay.reshape(1, row_block, input_count)
    return (bandpass, lags, delays)


def solution(mesh):
    in_specs = (P("stn", "pol", None, None), P("stn"), P(), P())
    out_specs = (
        P(("stn", "pol"), None),
        P(("stn", "pol"), None, None, None, None),
        P(("stn", "pol"), None, None),
    )
    return jax.shard_map(
        per_device, mesh=mesh, in_specs=in_specs, out_specs=out_specs, check_vma=False
    )
```

profile of v0, /device:TPU:0, one launch (start us, length us, event | category | flops | bytes accessed | tf_op | source)
XLA Modules:
  0.0 214.2 jit_solution(16711043971199102568)
XLA Ops:
  1.3 2.0 gather_fusion.1
  6.2 17.1 %while.14 = (s32[]{:T(128)}, bf16[4,1,2,132992]{3,2,1,0:T(2,128)(2,1)}, s32[4,4]{1,0:T(4,128)S(1)}, bf16[4,1,2,132864]{3,2,1,0:T(2,128)(2,1)}, s32[]{:T(128)}) while((s32[]{:T(128)}, bf16[4,1,2,132992]{3,2,1,0:T(2,128)(2,1)}, s32[4,4]{1,0:T(4,128)S(1)}, bf16[4,1,2,132864]{3,2,1,0:T(2,128)(2,1)}, s32[]{:T(128)}) %tuple.66), condition=%wide.while_cond, body=%wide.while_body.sunk | while | flops 2 | bytes 1064561 | solution.py:67
  6.8 3.7 %dynamic-slice_dynamic-update-slice_fusion.2 = bf16[4,1,2,132864]{3,2,1,0:T(2,128)(2,1)} fusion(bf16[4,1,2,132864]{3,2,1,0:T(2,128)(2,1)} %get-tuple-element.198, s32[]{:T(128)} %get-tuple-element.195, bf16[4,1,2,132992]{3,2,1,0:T(2,128)(2,1)} %get-tuple-element.201, s32[]{:T(128)} %bitcast.103, s32[]{:T(128)} %bitcast.104), kind=kLoop, calls=%fused_computation.4.clone.1 | loop fusion | bytes 1064448 | tf_op jit(solution)/shard_map/vmap()/gather
  11.1 3.7 %dynamic-slice_dynamic-update-slice_fusion.2 = bf16[4,1,2,132864]{3,2,1,0:T(2,128)(2,1)} fusion(bf16[4,1,2,132864]{3,2,1,0:T(2,128)(2,1)} %get-tuple-element.198, s32[]{:T(128)} %get-tuple-element.195, bf16[4,1,2,132992]{3,2,1,0:T(2,128)(2,1)} %get-tuple-element.201, s32[]{:T(128)} %bitcast.103, s32[]{:T(128)} %bitcast.104), kind=kLoop, calls=%fused_computation.4.clone.1 | loop fusion | bytes 1064448 | tf_op jit(solution)/shard_map/vmap()/gather
  15.4 3.7 %dynamic-slice_dynamic-update-slice_fusion.2 = bf16[4,1,2,132864]{3,2,1,0:T(2,128)(2,1)} fusion(bf16[4,1,2,132864]{3,2,1,0:T(2,128)(2,1)} %get-tuple-element.198, s32[]{:T(128)} %get-tuple-element.195, bf16[4,1,2,132992]{3,2,1,0:T(2,128)(2,1)} %get-tuple-element.201, s32[]{:T(128)} %bitcast.103, s32[]{:T(128)} %bitcast.104), kind=kLoop, calls=%fused_computation.4.clone.1 | loop fusion | bytes 1064448 | tf_op jit(solution)/shard_map/vmap()/gather
  19.6 3.7 %dynamic-slice_dynamic-update-slice_fusion.2 = bf16[4,1,2,132864]{3,2,1,0:T(2,128)(2,1)} fusion(bf16[4,1,2,132864]{3,2,1,0:T(2,128)(2,1)} %get-tuple-element.198, s32[]{:T(128)} %get-tuple-element.195, bf16[4,1,2,132992]{3,2,1,0:T(2,128)(2,1)} %get-tuple-element.201, s32[]{:T(128)} %bitcast.103, s32[]{:T(128)} %bitcast.104), kind=kLoop, calls=%fused_computation.4.clone.1 | loop fusion | bytes 1064448 | tf_op jit(solution)/shard_map/vmap()/gather
  23.3 4.8 %reshape.434 = bf16[4,1,2,519,256]{4,3,2,0,1:T(8,128)(2,1)S(1)} reshape(bf16[4,1,2,132864]{3,2,1,0:T(2,128)(2,1)} %get-tuple-element.40) | data formatting | bytes 4251648 | tf_op jit(solution)/shard_map/reshape | solution.py:45
  28.2 5.6 %fusion.8 = bf16[4,1,2,256,512]{3,4,2,0,1:T(8,128)(2,1)} fusion(f32[256]{0:T(256)S(1)} %get-tuple-element.103, bf16[4,1,2,519,256]{4,3,2,0,1:T(8,128)(2,1)S(1)} %reshape.434, f32[256]{0:T(256)S(1)} %get-tuple-element.104, f32[256]{0:T(256)S(1)} %get-tuple-element.105, f32[256]{0:T(256)S(1)} %get-tuple-element.106, f32[256]{0:T(256)S(1)} %get-tuple-element.107, ...), kind=kOutput, calls=%fused_computation.25 | convolution fusion | flops 1101004800 | bytes 19406848 | tf_op jit(solution)/shard_map/qkpc,tapsc->taqks/dot_general | solution.py:71
  33.8 4.9 %copy.25 = bf16[4,1,2,256,512]{4,2,0,1,3:T(2,128)(2,1)S(1)} copy(bf16[4,1,2,256,512]{3,4,2,0,1:T(8,128)(2,1)} %fusion.8) | data formatting | bytes 4194304 | tf_op jit(solution)/shard_map/convert_element_type | solution.py:73
  38.7 54.4 %all_to_all.69 = bf16[4,1,2,256,512]{4,2,0,1,3:T(2,128)(2,1)S(1)} all-to-all(bf16[4,1,2,256,512]{4,2,0,1,3:T(2,128)(2,1)S(1)} %copy.25), channel_id=1, replica_groups=mesh['stn'=16,'pol'=2] {'stn'}, dimensions={3} | all-to-all | bytes 4194304 | tf_op jit(solution)/shard_map/all_to_all | solution.py:75
  94.1 3.5 %copy.28 = bf16[64,1,2,16,512]{4,2,0,1,3:T(2,128)(2,1)} copy(bf16[64,1,2,16,512]{4,3,2,0,1:T(8,128)(2,1)S(1)} %bitcast.106) | data formatting | bytes 4194304 | tf_op jit(solution)/shard_map/all_to_all | solution.py:75
  97.6 3.9 %all-to-all-start.1 = ((bf16[64,1,2,16,512]{4,2,0,1,3:T(2,128)(2,1)}), bf16[64,1,2,16,512]{4,2,0,1,3:T(2,128)(2,1)S(1)}, u32[]{:S(2)}, u32[]{:S(2)}) async-start(bf16[64,1,2,16,512]{4,2,0,1,3:T(2,128)(2,1)} %copy.28), calls=%async_computation.1 | async-start | bytes 4194304 | tf_op jit(solution)/shard_map/all_to_all | solution.py:74
  102.5 25.1 %all-to-all-done.1 = bf16[64,1,2,16,512]{4,2,0,1,3:T(2,128)(2,1)S(1)} async-done(((bf16[64,1,2,16,512]{4,2,0,1,3:T(2,128)(2,1)}), bf16[64,1,2,16,512]{4,2,0,1,3:T(2,128)(2,1)S(1)}, u32[]{:S(2)}, u32[]{:S(2)}) %all-to-all-start.1) | async-done | bytes 2097184 | tf_op jit(solution)/shard_map/all_to_all | solution.py:74
  127.6 2.2 %copy.41 = bf16[64,1,2,16,512]{4,3,2,0,1:T(8,128)(2,1)S(1)} copy(bf16[64,1,2,16,512]{4,2,0,1,3:T(2,128)(2,1)S(1)} %all-to-all-done.1) | data formatting | bytes 4194304 | tf_op jit(solution)/shard_map/all_to_all | solution.py:74
  131.0 47.9 %while.13 = (s32[]{:T(128)}, bf16[8,2,128,128]{3,2,1,0:T(8,128)(2,1)S(1)}, f32[8,128]{1,0:T(8,128)}, s32[8]{0:T(128)S(1)}, bf16[64,2,2,8,512]{4,0,3,2,1:T(8,128)(2,1)S(1)}, /*index=5*/s32[]{:T(128)}, s32[]{:T(128)}, s32[]{:T(128)}) while((s32[]{:T(128)}, bf16[8,2,128,128]{3,2,1,0:T(8,128)(2,1)S(1)}, f32[8,128]{1,0:T(8,128)}, s32[8]{0:T(128)S(1)}, ...), condition=%wide.region_2.3_spmd, body=%wide.region_1.2_spmd.sunk | while | flops 69042688 | bytes 3804815 | solution.py:100
  135.7 1.3 dynamic_update_slice.12
  141.7 1.3 dynamic_update_slice.12
  147.7 1.3 dynamic_update_slice.12
  153.7 1.3 dynamic_update_slice.12
  159.7 1.3 dynamic_update_slice.12
  165.7 1.3 dynamic_update_slice.12
  180.3 18.6 %all_to_all.70 = bf16[1,1,8,2,128,128]{5,2,3,1,0,4:T(8,128)(2,1)S(1)} all-to-all(bf16[1,1,8,2,128,128]{5,2,3,1,0,4:T(8,128)(2,1)S(1)} %copy.33), channel_id=1, replica_groups=mesh['stn'=16,'pol'=2] {'stn'}, dimensions={4} | all-to-all | bytes 1048576 | tf_op jit(solution)/shard_map/all_to_all | solution.py:107
  199.9 3.5 %all-to-all-start.3 = ((bf16[16,1,8,2,8,128]{5,2,0,3,1,4:T(8,128)(2,1)}), bf16[16,1,8,2,8,128]{5,2,0,3,1,4:T(8,128)(2,1)S(1)}, u32[]{:S(2)}, u32[]{:S(2)}) async-start(bf16[16,1,8,2,8,128]{5,2,0,3,1,4:T(8,128)(2,1)} %bitcast.88), calls=%async_computation.3 | async-start | bytes 1048576 | tf_op jit(solution)/shard_map/all_to_all | solution.py:106
  204.6 7.3 %all-to-all-done.3 = bf16[16,1,8,2,8,128]{5,2,0,3,1,4:T(8,128)(2,1)S(1)} async-done(((bf16[16,1,8,2,8,128]{5,2,0,3,1,4:T(8,128)(2,1)}), bf16[16,1,8,2,8,128]{5,2,0,3,1,4:T(8,128)(2,1)S(1)}, u32[]{:S(2)}, u32[]{:S(2)}) %all-to-all-start.3) | async-done | bytes 524320 | tf_op jit(solution)/shard_map/all_to_all | solution.py:106
  (176 shorter events, 37.9 us)
Async XLA Ops:
  0.6 101.0 %copy-start = (s32[32]{0:T(128)S(1)}, s32[32]{0:T(128)}, u32[]{:S(2)}) copy-start(s32[32]{0:T(128)} %param.9) | copy-start | bytes 388
  97.6 30.0 %all-to-all-start.1 = ((bf16[64,1,2,16,512]{4,2,0,1,3:T(2,128)(2,1)}), bf16[64,1,2,16,512]{4,2,0,1,3:T(2,128)(2,1)S(1)}, u32[]{:S(2)}, u32[]{:S(2)}) async-start(bf16[64,1,2,16,512]{4,2,0,1,3:T(2,128)(2,1)} %copy.28), calls=%async_computation.1 | async-start | bytes 4194304 | tf_op jit(solution)/shard_map/all_to_all | solution.py:74
  180.2 23.2 %copy-start.1 = (s32[256]{0:T(256)S(1)}, s32[256]{0:T(256)}, u32[]{:S(2)}) copy-start(s32[256]{0:T(256)} %param.8) | copy-start | bytes 3076
  199.9 12.0 %all-to-all-start.3 = ((bf16[16,1,8,2,8,128]{5,2,0,3,1,4:T(8,128)(2,1)}), bf16[16,1,8,2,8,128]{5,2,0,3,1,4:T(8,128)(2,1)S(1)}, u32[]{:S(2)}, u32[]{:S(2)}) async-start(bf16[16,1,8,2,8,128]{5,2,0,3,1,4:T(8,128)(2,1)} %bitcast.88), calls=%async_computation.3 | async-start | bytes 1048576 | tf_op jit(solution)/shard_map/all_to_all | solution.py:106
where the time goes:
time: 215 us; the launch traced here: 214 us
  blocking collectives  73 us (34%)
  local copies, waits for them, and re-layouts  69.6 us (32%)
  waiting for transfers between devices  32.4 us (15%)
  loops' own time  16.3 us (8%)
  matrix products  8.48 us (4%)
  starting transfers between devices  7.43 us (3%)
  other arithmetic  5.45 us (3%)
    all_to_all x1, blocking collectives, per_device(): lax.all_to_all(spectra, 'stn', split_axis=3, concat_axis=0, tiled=True)  54.4 us
    all_to_all x1, waiting for transfers between devices, per_device(): lax.all_to_all(lax.all_to_all(spectra, 'stn', split_axis=3, concat_axis=0...  25.1 us
    all_to_all x1, blocking collectives, per_device(): lax.all_to_all(arranged, 'stn', split_axis=4, concat_axis=0, tiled=True)  18.6 us
    gather x12, local copies, waits for them, and re-layouts  17.1 us
    another operation x1, loops' own time, per_device(): lax.map(correlate, jnp.arange(local_channels, dtype=jnp.int32))  16.3 us
    dynamic_update_slice x8, local copies, waits for them, and re-layouts, per_device(): lax.map(correlate, jnp.arange(local_channels, dtype=jnp.int32))  10.4 us
    gather x8, local copies, waits for them, and re-layouts, correlate(): jnp.diagonal(vis_real)  9.96 us
    all_to_all x1, waiting for transfers between devices, per_device(): lax.all_to_all(lax.all_to_all(arranged, 'stn', split_axis=4, concat_axis=...  7.31 us
  transfers between devices with their start and end apart: 2, of which 2 were waited for; matrix products, arithmetic and copies ran while one was open for 1% of the time, Pallas kernels for 0%

commit v1 on v0

--- a/solution.py
+++ b/solution.py
@@ -7,6 +7,22 @@
 CHANNELS = 256
 TAPS = 8
 SPECTRA = 512
+
+
+def swapped_with_each(x, axis, split, join):
+    ways, here = (lax.axis_size(axis), lax.axis_index(axis))
+    width = x.shape[split] // ways
+    dims = list(x.shape)
+    dims[split] = width
+    height = dims[join]
+    dims[join] = height * ways
+    full = jnp.zeros(dims, x.dtype)
+    for mask in range(ways):
+        part = lax.dynamic_slice_in_dim(x, (here ^ mask) * width, width, axis=split)
+        if mask:
+            part = lax.ppermute(part, axis, [(d, d ^ mask) for d in range(ways)])
+        full = lax.dynamic_update_slice_in_dim(full, part, (here ^ mask) * height, axis=join)
+    return full
 
 
 def prototype():
@@ -104,11 +120,7 @@
     arranged = jnp.take(blocked, jnp.take(row_assign, block_index), axis=2)
     arranged = arranged.reshape(1, 1, local_channels, 2, input_count, input_count)
     regrouped = lax.all_to_all(
-        lax.all_to_all(arranged, "stn", split_axis=4, concat_axis=0, tiled=True),
-        "pol",
-        split_axis=4,
-        concat_axis=1,
-        tiled=True,
+        swapped_with_each(arranged, "stn", 4, 0), "pol", split_axis=4, concat_axis=1, tiled=True
     )
     gathered = regrouped.reshape(CHANNELS, 2, row_block * input_count)
     backward = lag_table(channel_map)

time: 215 us -> 229 us (1.065)
  starting transfers between devices: 7.43 us -> 27.9 us
  blocking collectives: 73 us -> 54.4 us
  local copies, waits for them, and re-layouts: 69.6 us -> 79.5 us
    ppermute x0 -> x15, starting transfers between devices: none -> 20.5 us  [swapped_with_each(): part = lax.ppermute(part, axis, [(d, d ^ mask) for d in range(ways)])]
    all_to_all x1 -> x0, blocking collectives: 18.6 us -> none  [per_device(): lax.all_to_all(arranged, 'stn', split_axis=4, concat_axis=0, tiled=True)]
    dynamic_update_slice x0 -> x16, local copies, waits for them, and re-layouts: none -> 9.92 us  [swapped_with_each(): lax.dynamic_update_slice_in_dim(full, part, (here ^ mask) * height, axis=...]
  transfers between devices with their start and end apart: 2 -> 17, of which waited for: 2 -> 3; matrix products, arithmetic and copies ran while one was open for 1% -> 5% of each run, Pallas kernels for 0% -> 0%
where the time goes in v1:
time: 229 us; the launch traced here: 228 us
  local copies, waits for them, and re-layouts  79.5 us (35%)
  blocking collectives  54.4 us (24%)
  waiting for transfers between devices  33.7 us (15%)
  starting transfers between devices  27.9 us (12%)
  loops' own time  16.3 us (7%)
  matrix products  8.44 us (4%)
  other arithmetic  5.47 us (2%)
    all_to_all x1, blocking collectives, per_device(): lax.all_to_all(spectra, 'stn', split_axis=3, concat_axis=0, tiled=True)  54.4 us
    all_to_all x1, waiting for transfers between devices, per_device(): lax.all_to_all(lax.all_to_all(spectra, 'stn', split_axis=3, concat_axis=0...  24.7 us
    ppermute x15, starting transfers between devices, swapped_with_each(): part = lax.ppermute(part, axis, [(d, d ^ mask) for d in range(ways)])  20.5 us
    gather x12, local copies, waits for them, and re-layouts  17.1 us
    another operation x1, loops' own time, per_device(): lax.map(correlate, jnp.arange(local_channels, dtype=jnp.int32))  16.3 us
    dynamic_update_slice x8, local copies, waits for them, and re-layouts, per_device(): lax.map(correlate, jnp.arange(local_channels, dtype=jnp.int32))  10.4 us
    gather x8, local copies, waits for them, and re-layouts, correlate(): jnp.diagonal(vis_real)  9.96 us
    dynamic_update_slice x16, local copies, waits for them, and re-layouts, swapped_with_each(): lax.dynamic_update_slice_in_dim(full, part, (here ^ mask) * height, axis=...  9.92 us
  transfers between devices with their start and end apart: 17, of which 3 were waited for; matrix products, arithmetic and copies ran while one was open for 5% of the time, Pallas kernels for 0%

profile of v1, /device:TPU:0, one launch (start us, length us, event | category | flops | bytes accessed | tf_op | source)
XLA Modules:
  0.0 227.7 jit_solution(1248690887181721612)
XLA Ops:
  1.3 2.0 gather_fusion.1
  6.2 17.1 %while.14 = (s32[]{:T(128)}, bf16[4,1,2,132992]{3,2,1,0:T(2,128)(2,1)}, s32[4,4]{1,0:T(4,128)S(1)}, bf16[4,1,2,132864]{3,2,1,0:T(2,128)(2,1)}, s32[]{:T(128)}) while((s32[]{:T(128)}, bf16[4,1,2,132992]{3,2,1,0:T(2,128)(2,1)}, s32[4,4]{1,0:T(4,128)S(1)}, bf16[4,1,2,132864]{3,2,1,0:T(2,128)(2,1)}, s32[]{:T(128)}) %tuple.81), condition=%wide.while_cond, body=%wide.while_body.sunk | while | flops 2 | bytes 1064561 | solution.py:83
  6.8 3.7 %dynamic-slice_dynamic-update-slice_fusion.2 = bf16[4,1,2,132864]{3,2,1,0:T(2,128)(2,1)} fusion(bf16[4,1,2,132864]{3,2,1,0:T(2,128)(2,1)} %get-tuple-element.214, s32[]{:T(128)} %get-tuple-element.211, bf16[4,1,2,132992]{3,2,1,0:T(2,128)(2,1)} %get-tuple-element.217, s32[]{:T(128)} %bitcast.97, s32[]{:T(128)} %bitcast.98), kind=kLoop, calls=%fused_computation.4.clone.1 | loop fusion | bytes 1064448 | tf_op jit(solution)/shard_map/vmap()/gather
  11.1 3.7 %dynamic-slice_dynamic-update-slice_fusion.2 = bf16[4,1,2,132864]{3,2,1,0:T(2,128)(2,1)} fusion(bf16[4,1,2,132864]{3,2,1,0:T(2,128)(2,1)} %get-tuple-element.214, s32[]{:T(128)} %get-tuple-element.211, bf16[4,1,2,132992]{3,2,1,0:T(2,128)(2,1)} %get-tuple-element.217, s32[]{:T(128)} %bitcast.97, s32[]{:T(128)} %bitcast.98), kind=kLoop, calls=%fused_computation.4.clone.1 | loop fusion | bytes 1064448 | tf_op jit(solution)/shard_map/vmap()/gather
  15.4 3.7 %dynamic-slice_dynamic-update-slice_fusion.2 = bf16[4,1,2,132864]{3,2,1,0:T(2,128)(2,1)} fusion(bf16[4,1,2,132864]{3,2,1,0:T(2,128)(2,1)} %get-tuple-element.214, s32[]{:T(128)} %get-tuple-element.211, bf16[4,1,2,132992]{3,2,1,0:T(2,128)(2,1)} %get-tuple-element.217, s32[]{:T(128)} %bitcast.97, s32[]{:T(128)} %bitcast.98), kind=kLoop, calls=%fused_computation.4.clone.1 | loop fusion | bytes 1064448 | tf_op jit(solution)/shard_map/vmap()/gather
  19.6 3.7 %dynamic-slice_dynamic-update-slice_fusion.2 = bf16[4,1,2,132864]{3,2,1,0:T(2,128)(2,1)} fusion(bf16[4,1,2,132864]{3,2,1,0:T(2,128)(2,1)} %get-tuple-element.214, s32[]{:T(128)} %get-tuple-element.211, bf16[4,1,2,132992]{3,2,1,0:T(2,128)(2,1)} %get-tuple-element.217, s32[]{:T(128)} %bitcast.97, s32[]{:T(128)} %bitcast.98), kind=kLoop, calls=%fused_computation.4.clone.1 | loop fusion | bytes 1064448 | tf_op jit(solution)/shard_map/vmap()/gather
  23.3 4.8 %reshape.434 = bf16[4,1,2,519,256]{4,3,2,0,1:T(8,128)(2,1)S(1)} reshape(bf16[4,1,2,132864]{3,2,1,0:T(2,128)(2,1)} %get-tuple-element.40) | data formatting | bytes 4251648 | tf_op jit(solution)/shard_map/reshape | solution.py:61
  28.2 5.5 %fusion.8 = bf16[4,1,2,256,512]{3,4,2,0,1:T(8,128)(2,1)} fusion(f32[256]{0:T(256)S(1)} %get-tuple-element.119, bf16[4,1,2,519,256]{4,3,2,0,1:T(8,128)(2,1)S(1)} %reshape.434, f32[256]{0:T(256)S(1)} %get-tuple-element.120, f32[256]{0:T(256)S(1)} %get-tuple-element.121, f32[256]{0:T(256)S(1)} %get-tuple-element.122, f32[256]{0:T(256)S(1)} %get-tuple-element.123, ...), kind=kOutput, calls=%fused_computation.25 | convolution fusion | flops 1101004800 | bytes 19406848 | tf_op jit(solution)/shard_map/qkpc,tapsc->taqks/dot_general | solution.py:87
  33.7 4.9 %copy.29 = bf16[4,1,2,256,512]{4,2,0,1,3:T(2,128)(2,1)S(1)} copy(bf16[4,1,2,256,512]{3,4,2,0,1:T(8,128)(2,1)} %fusion.8) | data formatting | bytes 4194304 | tf_op jit(solution)/shard_map/convert_element_type | solution.py:89
  38.7 54.4 %all_to_all.51 = bf16[4,1,2,256,512]{4,2,0,1,3:T(2,128)(2,1)S(1)} all-to-all(bf16[4,1,2,256,512]{4,2,0,1,3:T(2,128)(2,1)S(1)} %copy.29), channel_id=1, replica_groups=mesh['stn'=16,'pol'=2] {'stn'}, dimensions={3} | all-to-all | bytes 4194304 | tf_op jit(solution)/shard_map/all_to_all | solution.py:91
  94.0 3.5 %copy.32 = bf16[64,1,2,16,512]{4,2,0,1,3:T(2,128)(2,1)} copy(bf16[64,1,2,16,512]{4,3,2,0,1:T(8,128)(2,1)S(1)} %bitcast.100) | data formatting | bytes 4194304 | tf_op jit(solution)/shard_map/all_to_all | solution.py:91
  97.5 3.9 %all-to-all-start.1 = ((bf16[64,1,2,16,512]{4,2,0,1,3:T(2,128)(2,1)}), bf16[64,1,2,16,512]{4,2,0,1,3:T(2,128)(2,1)S(1)}, u32[]{:S(2)}, u32[]{:S(2)}) async-start(bf16[64,1,2,16,512]{4,2,0,1,3:T(2,128)(2,1)} %copy.32), calls=%async_computation.1 | async-start | bytes 4194304 | tf_op jit(solution)/shard_map/all_to_all | solution.py:90
  102.8 24.7 %all-to-all-done.1 = bf16[64,1,2,16,512]{4,2,0,1,3:T(2,128)(2,1)S(1)} async-done(((bf16[64,1,2,16,512]{4,2,0,1,3:T(2,128)(2,1)}), bf16[64,1,2,16,512]{4,2,0,1,3:T(2,128)(2,1)S(1)}, u32[]{:S(2)}, u32[]{:S(2)}) %all-to-all-start.1) | async-done | bytes 2097184 | tf_op jit(solution)/shard_map/all_to_all | solution.py:90
  127.5 2.2 copy.74
  130.9 48.0 %while.13 = (s32[]{:T(128)}, bf16[8,2,128,128]{3,2,1,0:T(8,128)(2,1)S(1)}, f32[8,128]{1,0:T(8,128)}, s32[8]{0:T(128)S(1)}, bf16[64,2,2,8,512]{4,0,3,2,1:T(8,128)(2,1)S(1)}, /*index=5*/s32[]{:T(128)}, s32[]{:T(128)}, s32[]{:T(128)}) while((s32[]{:T(128)}, bf16[8,2,128,128]{3,2,1,0:T(8,128)(2,1)S(1)}, f32[8,128]{1,0:T(8,128)}, s32[8]{0:T(128)S(1)}, ...), condition=%wide.region_2.3_spmd, body=%wide.region_1.2_spmd.sunk | while | flops 69042688 | bytes 3804815 | solution.py:116
  182.3 1.7 collective-permute-start.3
  185.6 2.1 collective-permute-start.5
  189.4 1.6 collective-permute-start.7
  193.3 2.0 collective-permute-start.9
  198.1 2.0 collective-permute-start.11
  202.9 3.1 %collective-permute-start.13 = (bf16[1,1,8,2,8,128]{5,2,4,3,1,0:T(8,128)(2,1)S(1)}, bf16[1,1,8,2,8,128]{5,2,4,3,1,0:T(8,128)(2,1)S(1)}, u32[]{:S(2)}, u32[]{:S(2)}) collective-permute-start(bf16[1,1,8,2,8,128]{5,2,4,3,1,0:T(8,128)(2,1)S(1)} %get-tuple-element.99), channel_id=1, source_target_pairs={{0,28},{2,30},{4,24},{6,26},{8,20},{10,22},{12,16},{14,18},{16,12}... | collective-permute-start | bytes 98312 | tf_op jit(solution)/shard_map/ppermute | solution.py:23
  211.1 1.6 collective-permute-done.14
  213.4 3.5 %all-to-all-start.2 = ((bf16[16,1,8,2,8,128]{5,2,0,3,1,4:T(8,128)(2,1)}), bf16[16,1,8,2,8,128]{5,2,0,3,1,4:T(8,128)(2,1)S(1)}, u32[]{:S(2)}, u32[]{:S(2)}) async-start(bf16[16,1,8,2,8,128]{5,2,0,3,1,4:T(8,128)(2,1)} %copy_dynamic-update-slice_fusion), calls=%async_computation.2 | async-start | bytes 1048576 | tf_op jit(solution)/shard_map/all_to_all | solution.py:122
  218.1 7.3 %all-to-all-done.2 = bf16[16,1,8,2,8,128]{5,2,0,3,1,4:T(8,128)(2,1)S(1)} async-done(((bf16[16,1,8,2,8,128]{5,2,0,3,1,4:T(8,128)(2,1)}), bf16[16,1,8,2,8,128]{5,2,0,3,1,4:T(8,128)(2,1)S(1)}, u32[]{:S(2)}, u32[]{:S(2)}) %all-to-all-start.2) | async-done | bytes 524320 | tf_op jit(solution)/shard_map/all_to_all | solution.py:122
  (221 shorter events, 63.6 us)
Async XLA Ops:
  0.6 101.1 %copy-start = (s32[32]{0:T(128)S(1)}, s32[32]{0:T(128)}, u32[]{:S(2)}) copy-start(s32[32]{0:T(128)} %param.9) | copy-start | bytes 388
  97.5 30.0 %all-to-all-start.1 = ((bf16[64,1,2,16,512]{4,2,0,1,3:T(2,128)(2,1)}), bf16[64,1,2,16,512]{4,2,0,1,3:T(2,128)(2,1)S(1)}, u32[]{:S(2)}, u32[]{:S(2)}) async-start(bf16[64,1,2,16,512]{4,2,0,1,3:T(2,128)(2,1)} %copy.32), calls=%async_computation.1 | async-start | bytes 4194304 | tf_op jit(solution)/shard_map/all_to_all | solution.py:90
  180.0 36.9 %copy-start.1 = (s32[256]{0:T(256)S(1)}, s32[256]{0:T(256)}, u32[]{:S(2)}) copy-start(s32[256]{0:T(256)} %param.8) | copy-start | bytes 3076
  180.4 5.2 %collective-permute-start = (bf16[1,1,8,2,8,128]{5,2,4,3,1,0:T(8,128)(2,1)S(1)}, bf16[1,1,8,2,8,128]{5,2,4,3,1,0:T(8,128)(2,1)S(1)}, u32[]{:S(2)}, u32[]{:S(2)}) collective-permute-start(bf16[1,1,8,2,8,128]{5,2,4,3,1,0:T(8,128)(2,1)S(1)} %get-tuple-element.112), channel_id=1, source_target_pairs={{0,2},{2,0},{4,6},{6,4},{8,10},{10,8},{12,14},{14,12},{16,18},{18,... | collective-permute-start | bytes 98312 | tf_op jit(solution)/shard_map/ppermute | solution.py:23
  180.5 7.7 %collective-permute-start.1 = (bf16[1,1,8,2,8,128]{5,2,4,3,1,0:T(8,128)(2,1)S(1)}, bf16[1,1,8,2,8,128]{5,2,4,3,1,0:T(8,128)(2,1)S(1)}, u32[]{:S(2)}, u32[]{:S(2)}) collective-permute-start(bf16[1,1,8,2,8,128]{5,2,4,3,1,0:T(8,128)(2,1)S(1)} %get-tuple-element.111), channel_id=1, source_target_pairs={{0,4},{2,6},{4,0},{6,2},{8,12},{10,14},{12,8},{14,10},{16,20},{18,... | collective-permute-start | bytes 98312 | tf_op jit(solution)/shard_map/ppermute | solution.py:23
  181.8 7.6 %collective-permute-start.2 = (bf16[1,1,8,2,8,128]{5,2,4,3,1,0:T(8,128)(2,1)S(1)}, bf16[1,1,8,2,8,128]{5,2,4,3,1,0:T(8,128)(2,1)S(1)}, u32[]{:S(2)}, u32[]{:S(2)}) collective-permute-start(bf16[1,1,8,2,8,128]{5,2,4,3,1,0:T(8,128)(2,1)S(1)} %get-tuple-element.110), channel_id=1, source_target_pairs={{0,6},{2,4},{4,2},{6,0},{8,14},{10,12},{12,10},{14,8},{16,22},{18,... | collective-permute-start | bytes 98312 | tf_op jit(solution)/shard_map/ppermute | solution.py:23
  182.3 9.4 %collective-permute-start.3 = (bf16[1,1,8,2,8,128]{5,2,4,3,1,0:T(8,128)(2,1)S(1)}, bf16[1,1,8,2,8,128]{5,2,4,3,1,0:T(8,128)(2,1)S(1)}, u32[]{:S(2)}, u32[]{:S(2)}) collective-permute-start(bf16[1,1,8,2,8,128]{5,2,4,3,1,0:T(8,128)(2,1)S(1)} %get-tuple-element.109), channel_id=1, source_target_pairs={{0,8},{2,10},{4,12},{6,14},{8,0},{10,2},{12,4},{14,6},{16,24},{18,... | collective-permute-start | bytes 98312 | tf_op jit(solution)/shard_map/ppermute | solution.py:23
  184.0 9.3 %collective-permute-start.4 = (bf16[1,1,8,2,8,128]{5,2,4,3,1,0:T(8,128)(2,1)S(1)}, bf16[1,1,8,2,8,128]{5,2,4,3,1,0:T(8,128)(2,1)S(1)}, u32[]{:S(2)}, u32[]{:S(2)}) collective-permute-start(bf16[1,1,8,2,8,128]{5,2,4,3,1,0:T(8,128)(2,1)S(1)} %get-tuple-element.108), channel_id=1, source_target_pairs={{0,10},{2,8},{4,14},{6,12},{8,2},{10,0},{12,6},{14,4},{16,26},{18,... | collective-permute-start | bytes 98312 | tf_op jit(solution)/shard_map/ppermute | solution.py:23
  185.6 10.4 %collective-permute-start.5 = (bf16[1,1,8,2,8,128]{5,2,4,3,1,0:T(8,128)(2,1)S(1)}, bf16[1,1,8,2,8,128]{5,2,4,3,1,0:T(8,128)(2,1)S(1)}, u32[]{:S(2)}, u32[]{:S(2)}) collective-permute-start(bf16[1,1,8,2,8,128]{5,2,4,3,1,0:T(8,128)(2,1)S(1)} %get-tuple-element.107), channel_id=1, source_target_pairs={{0,12},{2,14},{4,8},{6,10},{8,4},{10,6},{12,0},{14,2},{16,28},{18,... | collective-permute-start | bytes 98312 | tf_op jit(solution)/shard_map/ppermute | solution.py:23
  188.2 9.9 %collective-permute-start.6 = (bf16[1,1,8,2,8,128]{5,2,4,3,1,0:T(8,128)(2,1)S(1)}, bf16[1,1,8,2,8,128]{5,2,4,3,1,0:T(8,128)(2,1)S(1)}, u32[]{:S(2)}, u32[]{:S(2)}) collective-permute-start(bf16[1,1,8,2,8,128]{5,2,4,3,1,0:T(8,128)(2,1)S(1)} %get-tuple-element.106), channel_id=1, source_target_pairs={{0,14},{2,12},{4,10},{6,8},{8,6},{10,4},{12,2},{14,0},{16,30},{18,... | collective-permute-start | bytes 98312 | tf_op jit(solution)/shard_map/ppermute | solution.py:23
  189.4 11.3 %collective-permute-start.7 = (bf16[1,1,8,2,8,128]{5,2,4,3,1,0:T(8,128)(2,1)S(1)}, bf16[1,1,8,2,8,128]{5,2,4,3,1,0:T(8,128)(2,1)S(1)}, u32[]{:S(2)}, u32[]{:S(2)}) collective-permute-start(bf16[1,1,8,2,8,128]{5,2,4,3,1,0:T(8,128)(2,1)S(1)} %get-tuple-element.105), channel_id=1, source_target_pairs={{0,16},{2,18},{4,20},{6,22},{8,24},{10,26},{12,28},{14,30},{16,0},... | collective-permute-start | bytes 98312 | tf_op jit(solution)/shard_map/ppermute | solution.py:23
  191.7 11.2 %collective-permute-start.8 = (bf16[1,1,8,2,8,128]{5,2,4,3,1,0:T(8,128)(2,1)S(1)}, bf16[1,1,8,2,8,128]{5,2,4,3,1,0:T(8,128)(2,1)S(1)}, u32[]{:S(2)}, u32[]{:S(2)}) collective-permute-start(bf16[1,1,8,2,8,128]{5,2,4,3,1,0:T(8,128)(2,1)S(1)} %get-tuple-element.104), channel_id=1, source_target_pairs={{0,18},{2,16},{4,22},{6,20},{8,26},{10,24},{12,30},{14,28},{16,2},... | collective-permute-start | bytes 98312 | tf_op jit(solution)/shard_map/ppermute | solution.py:23
  193.3 13.4 %collective-permute-start.9 = (bf16[1,1,8,2,8,128]{5,2,4,3,1,0:T(8,128)(2,1)S(1)}, bf16[1,1,8,2,8,128]{5,2,4,3,1,0:T(8,128)(2,1)S(1)}, u32[]{:S(2)}, u32[]{:S(2)}) collective-permute-start(bf16[1,1,8,2,8,128]{5,2,4,3,1,0:T(8,128)(2,1)S(1)} %get-tuple-element.103), channel_id=1, source_target_pairs={{0,20},{2,22},{4,16},{6,18},{8,28},{10,30},{12,24},{14,26},{16,4},... | collective-permute-start | bytes 98312 | tf_op jit(solution)/shard_map/ppermute | solution.py:23
  196.0 12.6 %collective-permute-start.10 = (bf16[1,1,8,2,8,128]{5,2,4,3,1,0:T(8,128)(2,1)S(1)}, bf16[1,1,8,2,8,128]{5,2,4,3,1,0:T(8,128)(2,1)S(1)}, u32[]{:S(2)}, u32[]{:S(2)}) collective-permute-start(bf16[1,1,8,2,8,128]{5,2,4,3,1,0:T(8,128)(2,1)S(1)} %get-tuple-element.102), channel_id=1, source_target_pairs={{0,22},{2,20},{4,18},{6,16},{8,30},{10,28},{12,26},{14,24},{16,6},... | collective-permute-start | bytes 98312 | tf_op jit(solution)/shard_map/ppermute | solution.py:23
  198.1 11.1 %collective-permute-start.11 = (bf16[1,1,8,2,8,128]{5,2,4,3,1,0:T(8,128)(2,1)S(1)}, bf16[1,1,8,2,8,128]{5,2,4,3,1,0:T(8,128)(2,1)S(1)}, u32[]{:S(2)}, u32[]{:S(2)}) collective-permute-start(bf16[1,1,8,2,8,128]{5,2,4,3,1,0:T(8,128)(2,1)S(1)} %get-tuple-element.101), channel_id=1, source_target_pairs={{0,24},{2,26},{4,28},{6,30},{8,16},{10,18},{12,20},{14,22},{16,8},... | collective-permute-start | bytes 98312 | tf_op jit(solution)/shard_map/ppermute | solution.py:23
  200.8 9.1 %collective-permute-start.12 = (bf16[1,1,8,2,8,128]{5,2,4,3,1,0:T(8,128)(2,1)S(1)}, bf16[1,1,8,2,8,128]{5,2,4,3,1,0:T(8,128)(2,1)S(1)}, u32[]{:S(2)}, u32[]{:S(2)}) collective-permute-start(bf16[1,1,8,2,8,128]{5,2,4,3,1,0:T(8,128)(2,1)S(1)} %get-tuple-element.100), channel_id=1, source_target_pairs={{0,26},{2,24},{4,30},{6,28},{8,18},{10,16},{12,22},{14,20},{16,10}... | collective-permute-start | bytes 98312 | tf_op jit(solution)/shard_map/ppermute | solution.py:23
  202.9 7.6 %collective-permute-start.13 = (bf16[1,1,8,2,8,128]{5,2,4,3,1,0:T(8,128)(2,1)S(1)}, bf16[1,1,8,2,8,128]{5,2,4,3,1,0:T(8,128)(2,1)S(1)}, u32[]{:S(2)}, u32[]{:S(2)}) collective-permute-start(bf16[1,1,8,2,8,128]{5,2,4,3,1,0:T(8,128)(2,1)S(1)} %get-tuple-element.99), channel_id=1, source_target_pairs={{0,28},{2,30},{4,24},{6,26},{8,20},{10,22},{12,16},{14,18},{16,12}... | collective-permute-start | bytes 98312 | tf_op jit(solution)/shard_map/ppermute | solution.py:23
  206.7 6.1 %collective-permute-start.14 = (bf16[1,1,8,2,8,128]{5,2,4,3,1,0:T(8,128)(2,1)S(1)}, bf16[1,1,8,2,8,128]{5,2,4,3,1,0:T(8,128)(2,1)S(1)}, u32[]{:S(2)}, u32[]{:S(2)}) collective-permute-start(bf16[1,1,8,2,8,128]{5,2,4,3,1,0:T(8,128)(2,1)S(1)} %get-tuple-element.98), channel_id=1, source_target_pairs={{0,30},{2,28},{4,26},{6,24},{8,22},{10,20},{12,18},{14,16},{16,14}... | collective-permute-start | bytes 98312 | tf_op jit(solution)/shard_map/ppermute | solution.py:23
  213.4 12.1 %all-to-all-start.2 = ((bf16[16,1,8,2,8,128]{5,2,0,3,1,4:T(8,128)(2,1)}), bf16[16,1,8,2,8,128]{5,2,0,3,1,4:T(8,128)(2,1)S(1)}, u32[]{:S(2)}, u32[]{:S(2)}) async-start(bf16[16,1,8,2,8,128]{5,2,0,3,1,4:T(8,128)(2,1)} %copy_dynamic-update-slice_fusion), calls=%async_computation.2 | async-start | bytes 1048576 | tf_op jit(solution)/shard_map/all_to_all | solution.py:122
